TPU v7x, 256 devices: a whole 4x4x8 slice. The times are simulated.
256 devices in a mesh: tiles: 32 (over z, x), sub: 8 (over y, core).
Axes of the slice: x: 4, y: 4, z: 8, core: 2. Of those that a mesh axis runs over, the one named last changes fastest.
Arguments:
- latents: float32 [196608, 512], P(('tiles', 'sub')), may hold values from -130 to 130
- conv_weight: float32 [512, 9, 512], P('tiles'), may hold values from -0.09375 to 0.09375
- conv_bias: float32 [512], replicated, may hold values from -4 to 4
- norm1_gain: float32 [512], replicated, may hold values from 0.5 to 1.5
- norm1_shift: float32 [512], replicated, may hold values from -3 to 3
- norm2_gain: float32 [512], replicated, may hold values from 0.5 to 1.5
- norm2_shift: float32 [512], replicated, may hold values from -3 to 3
- tile_counts: int32 [36], replicated, may hold values from 1 to 64, 768 in all
- widths: int32 [36], replicated, may hold values from 32 to 128, as said below
Outputs:
- activated: float32 [196608, 512], P(('tiles', 'sub'))
Inputs may be any that keep to these rules, and one draw needn't show every extreme that they name: `widths`: each width is 128, 64 or 32; some image has width 128 and some has width 128 / 4. `tile_counts`: they add up to 768; the largest is 64.
All inputs are finite; a program needn't handle non-finite values.
Results may differ from a plain program's by a relative error of at most 0.00014.
Values sent between devices are 32-bit elements; how exact they have to be, the bound alone decides.
A program may use at most 128 MiB of HBM per device.

v0:
```python
import jax
import jax.numpy as jnp
from jax import lax
from jax.sharding import PartitionSpec as P

GROUPS = 32
WMAX = 128
TILE = 256
epsilon = 1e-06
highest = lax.Precision.HIGHEST


def extended(cells, sides, width):
    for axis, dim in sides:
        count = lax.axis_size(axis)
        ends = count - 1
        head = lax.slice_in_dim(cells, 0, width, axis=dim)
        tail = lax.slice_in_dim(cells, cells.shape[dim] - width, cells.shape[dim], axis=dim)
        cells = jnp.concatenate(
            [
                lax.ppermute(tail, axis, [(i, (i + 1) % count) for i in range(ends)]),
                cells,
                lax.ppermute(head, axis, [((i + 1) % count, i) for i in range(ends)]),
            ],
            axis=dim,
        )
    return cells


def pixel_layout(tile_counts, widths, pixels_here):
    device = lax.axis_index("tiles") * lax.axis_size("sub") + lax.axis_index("sub")
    pixel_counts = tile_counts * TILE
    image_ends = jnp.cumsum(pixel_counts)
    image_starts = image_ends - pixel_counts
    position = device * pixels_here + jnp.arange(pixels_here, dtype=jnp.int32)
    member = (position[None, :] >= image_starts[:, None]) & (
        position[None, :] < image_ends[:, None]
    )

    def per_pixel(per_image):
        return jnp.sum(jnp.where(member, per_image[:, None], 0), axis=0)

    pixel_width = per_pixel(widths)
    offset = position - per_pixel(image_starts)
    row_index = offset // pixel_width
    column_index = offset - row_index * pixel_width
    pixel_height = per_pixel(pixel_counts) // pixel_width
    return (
        member.astype(jnp.float32),
        pixel_counts,
        row_index,
        column_index,
        pixel_width,
        pixel_height,
    )


def group_table(per_channel):
    return jnp.sum(per_channel.reshape(per_channel.shape[0], GROUPS, -1), axis=2)


def spread_rows(onehot, per_image):
    return lax.dot_general(
        onehot,
        per_image,
        (((0,), (0,)), ((), ())),
        precision=highest,
        preferred_element_type=jnp.float32,
    )


def normalize(values, norm_gain, norm_shift, onehot, pixel_counts):
    group_size = values.shape[1] // GROUPS
    entries = (pixel_counts * group_size).astype(jnp.float32)[:, None]
    firsts = jnp.dot(onehot, values, precision=highest, preferred_element_type=jnp.float32)
    group_total = lax.psum(group_table(firsts), ("tiles", "sub"))
    group_mean = group_total / entries
    centred = values - spread_rows(onehot, jnp.repeat(group_mean, group_size, axis=1))
    seconds = jnp.dot(
        onehot, centred * centred, precision=highest, preferred_element_type=jnp.float32
    )
    spread = lax.psum(group_table(seconds), ("tiles", "sub")) / entries
    inverse = spread_rows(onehot, jnp.repeat(lax.rsqrt(spread + epsilon), group_size, axis=1))
    return jax.nn.silu(centred * inverse * norm_gain + norm_shift)


def shards(
    latents,
    conv_weight,
    conv_bias,
    norm1_gain,
    norm1_shift,
    norm2_gain,
    norm2_shift,
    tile_counts,
    widths,
):
    pixels_here = latents.shape[0]
    channels = latents.shape[1]
    onehot, pixel_counts, row_index, column_index, pixel_width, pixel_height = pixel_layout(
        tile_counts, widths, pixels_here
    )
    first_act = normalize(latents, norm1_gain, norm1_shift, onehot, pixel_counts)
    padded = extended(first_act.T, ((("tiles", "sub"), 1),), WMAX + 1)
    anchor = jnp.arange(pixels_here, dtype=jnp.int32) + (WMAX + 1)
    sources = []
    validity = []
    for step_y in (-1, 0, 1):
        for step_x in (-1, 0, 1):
            inside = (row_index + step_y >= 0) & (row_index + step_y < pixel_height)
            inside = inside & (column_index + step_x >= 0) & (column_index + step_x < pixel_width)
            sources.append(jnp.where(inside, anchor + step_y * pixel_width + step_x, anchor))
            validity.append(inside.astype(jnp.float32))
    all_sources = jnp.concatenate(sources)
    all_masks = jnp.concatenate(validity)
    tapped = jnp.take(padded, all_sources, axis=1) * all_masks[None, :]
    zero_sum = jnp.zeros((pixels_here, channels), jnp.float32)
    running = zero_sum
    weight_piece = lax.all_gather(conv_weight, "tiles", axis=0, tiled=True)
    row_count = weight_piece.shape[0]
    block_width = min(row_count, 128)
    for block_start in range(0, row_count, block_width):
        block_rows = min(block_width, row_count - block_start)
        taps_block = lax.dynamic_slice_in_dim(tapped, block_start, block_rows, 0)
        taps_block = taps_block.reshape(block_rows, 9, pixels_here)
        weight_block = weight_piece[block_start : block_start + block_rows]
        running = running + jnp.einsum(
            "ktp,kto->po",
            taps_block,
            weight_block,
            precision=highest,
            preferred_element_type=jnp.float32,
        )
    hidden = running
    hidden = hidden + conv_bias
    return normalize(hidden, norm2_gain, norm2_shift, onehot, pixel_counts)


def solution(mesh):
    return jax.shard_map(
        shards,
        mesh=mesh,
        in_specs=(
            P(("tiles", "sub"), None),
            P("tiles", None, None),
            P(),
            P(),
            P(),
            P(),
            P(),
            P(),
            P(),
        ),
        out_specs=P(("tiles", "sub"), None),
        check_vma=False,
    )
```

profile of v0, /device:TPU:1, one launch (start us, length us, event | category | flops | bytes accessed | tf_op | source)
XLA Modules:
  0.0 427.4 jit_solution(8447993397408596706)
XLA Ops:
  6.5 0.7 all-gather.2.cloned.1.call-update
  7.3 0.7 broadcast_multiply_fusion
  8.2 0.7 fusion.25
  8.9 2.8 bitcast_reduce_fusion.3
  11.7 83.9 %psum.28 = f32[36,32]{0,1:T(8,128)S(1)} all-reduce(f32[36,32]{0,1:T(8,128)S(1)} %bitcast_reduce_fusion.3), channel_id=1, replica_groups=mesh['tiles'=32,'sub'=8] {'tiles','sub'}, use_global_device_ids=true, to_apply=%region_5.6 | all-reduce | flops 1152 | bytes 9216 | tf_op jit(solution)/shard_map/psum | solution.py:76
  95.6 0.9 convolution_subtract_fusion.1
  96.6 1.4 bitcast_reduce_fusion.2
  98.0 73.4 %psum.29 = f32[36,32]{0,1:T(8,128)S(1)} all-reduce(f32[36,32]{0,1:T(8,128)S(1)} %bitcast_reduce_fusion.2), channel_id=1, replica_groups=mesh['tiles'=32,'sub'=8] {'tiles','sub'}, use_global_device_ids=true, to_apply=%region_7.8 | all-reduce | flops 1152 | bytes 9216 | tf_op jit(solution)/shard_map/psum | solution.py:82
  171.5 1.3 multiply_bitcast_fusion.1
  172.8 1.1 copy-done.4
  174.0 3.2 collective-permute-start
  177.2 2.4 collective-permute-start.1
  179.9 0.2 dynamic-update-slice
  180.1 0.2 dynamic-update-slice.1
  180.8 0.2 dynamic-update-slice.3
  181.3 0.2 dynamic-update-slice.5
  181.6 0.2 dynamic-update-slice.6
  182.4 2.6 collective-permute-done.1
  185.0 4.5 %concatenate.54 = f32[512,1026]{0,1:T(8,128)S(1)} concatenate(f32[512,129]{0,1:T(8,128)S(1)} %collective-permute-done, f32[512,768]{0,1:T(8,128)} %copy-done.4, f32[512,129]{0,1:T(8,128)S(1)} %collective-permute-done.1), dimensions={1} | concatenate | bytes 4202496 | tf_op jit(solution)/shard_map/concatenate | solution.py:19
  189.5 18.6 %gather_fusion = f32[6912,512]{1,0:T(8,128)} fusion(f32[512,1026]{0,1:T(8,128)S(1)} %concatenate.54, s32[7168]{0:T(1024)S(1)} %pad_clamp_fusion), kind=kCustom, calls=%fused_computation | custom fusion | bytes 28339200 | tf_op jit(solution)/shard_map/jit(_take)/gather | solution.py:116
  208.1 11.6 %multiply_bitcast_fusion = f32[512,6912]{0,1:T(8,128)} fusion(f32[6912,512]{1,0:T(8,128)} %gather_fusion, f32[6912]{0:T(1024)S(1)} %concatenate.66, pred[6912]{0:T(1024)(128)(4,1)S(1)} %compare_and_fusion.1), kind=kLoop, calls=%fused_computation.1 | loop fusion | flops 7077888 | bytes 28346112 | tf_op jit(solution)/shard_map/mul | solution.py:116
  219.7 9.4 %fusion.35 = (f32[128,6912]{0,1:T(8,128)}, f32[128,6912]{0,1:T(8,128)}, f32[128,6912]{0,1:T(8,128)}, f32[128,6912]{0,1:T(8,128)S(1)}) fusion(f32[512,6912]{0,1:T(8,128)} %multiply_bitcast_fusion), kind=kLoop, calls=%fused_computation.106 | loop fusion | bytes 28311552 | tf_op jit(solution)/shard_map/dynamic_slice | solution.py:124
  229.1 9.2 %fusion = f32[768,512,1]{1,0,2:T(8,128)S(1)} fusion(f32[128,9,768]{0,2,1:T(8,128)} %bitcast.48, f32[512,9,512]{2,0,1:T(8,128)} %all-gather.2.cloned.1.call-done), kind=kOutput, calls=%fused_computation.2 | convolution fusion | flops 5435817984 | bytes 7471104 | tf_op jit(solution)/shard_map/ktp,kto->po/dot_general | solution.py:127
  238.2 8.0 %fusion.2 = f32[768,512,1]{1,0,2:T(8,128)S(1)} fusion(f32[128,9,768]{0,2,1:T(8,128)S(1)} %bitcast.47, f32[512,9,512]{2,0,1:T(8,128)} %all-gather.2.cloned.1.call-done), kind=kOutput, calls=%fused_computation.4 | convolution fusion | flops 5435817984 | bytes 7471104 | tf_op jit(solution)/shard_map/ktp,kto->po/dot_general | solution.py:127
  246.3 6.5 %fusion.4 = f32[768,512,1]{1,0,2:T(8,128)S(1)} fusion(f32[128,9,768]{0,2,1:T(8,128)S(1)} %bitcast.46, f32[512,9,512]{2,0,1:T(8,128)S(1)} %copy-done.2), kind=kOutput, calls=%fused_computation.6 | convolution fusion | flops 5435817984 | bytes 7471104 | tf_op jit(solution)/shard_map/ktp,kto->po/dot_general | solution.py:127
  252.8 6.4 %fusion.8 = f32[768,512]{1,0:T(8,128)S(1)} fusion(f32[768,512,1]{1,0,2:T(8,128)S(1)} %fusion, f32[768,512,1]{1,0,2:T(8,128)S(1)} %fusion.2, f32[768,512,1]{1,0,2:T(8,128)S(1)} %fusion.4, f32[128,9,768]{0,2,1:T(8,128)S(1)} %bitcast.49, f32[512,9,512]{2,0,1:T(8,128)S(1)} %copy-done.2, f32[512]{0:T(512)S(1)} %copy-done.5), kind=kOutput, calls=%fused_computation.11 | convolution fusion | flops 5437390848 | bytes 12191744 | tf_op jit(solution)/shard_map/ktp,kto->po/dot_general | solution.py:127
  259.2 1.4 bitcast_reduce_fusion.1
  260.6 82.0 %psum.30 = f32[36,32]{0,1:T(8,128)S(1)} all-reduce(f32[36,32]{0,1:T(8,128)S(1)} %bitcast_reduce_fusion.1), channel_id=1, replica_groups=mesh['tiles'=32,'sub'=8] {'tiles','sub'}, use_global_device_ids=true, to_apply=%region_9.10 | all-reduce | flops 1152 | bytes 9216 | tf_op jit(solution)/shard_map/psum | solution.py:76
  342.6 0.9 convolution_subtract_fusion
  343.6 1.4 bitcast_reduce_fusion
  345.0 72.8 %psum.31 = f32[36,32]{0,1:T(8,128)S(1)} all-reduce(f32[36,32]{0,1:T(8,128)S(1)} %bitcast_reduce_fusion), channel_id=1, replica_groups=mesh['tiles'=32,'sub'=8] {'tiles','sub'}, use_global_device_ids=true, to_apply=%region_11.12 | all-reduce | flops 1152 | bytes 9216 | tf_op jit(solution)/shard_map/psum | solution.py:82
  417.9 2.4 divide_multiply_fusion
  (69 shorter events, 2.0 us)
Async XLA Ops:
  6.5 89.1 %copy-start.3 = (f32[768,512]{1,0:T(8,128)S(1)}, f32[768,512]{1,0:T(8,128)}, u32[]{:S(2)}) copy-start(f32[768,512]{1,0:T(8,128)} %param.9) | copy-start | bytes 4718596
  6.5 222.5 %all-gather.2.cloned.1.call-start = ((), (), s32[]{:S(2)}) async-start(), calls=%async_computation | async-start | bytes 9732096 | tf_op jit(solution)/shard_map/all_gather | solution.py:119
  96.6 74.9 %copy-start.7 = (f32[512]{0:T(512)S(1)}, f32[512]{0:T(512)}, u32[]{:S(2)}) copy-start(f32[512]{0:T(512)} %param.13) | copy-start | bytes 6148
  96.6 74.9 %copy-start.8 = (f32[512]{0:T(512)S(1)}, f32[512]{0:T(512)}, u32[]{:S(2)}) copy-start(f32[512]{0:T(512)} %param.12) | copy-start | bytes 6148
  171.5 8.1 %copy-start.6 = (s32[36]{0:T(128)S(1)}, s32[36]{0:T(128)}, u32[]{:S(2)}) copy-start(s32[36]{0:T(128)} %param.17) | copy-start | bytes 436
  172.8 1.1 copy-start.4
  174.0 8.5 %collective-permute-start = (f32[512,129]{0,1:T(8,128)S(1)}, f32[512,129]{0,1:T(8,128)S(1)}, u32[]{:S(2)}, u32[]{:S(2)}) collective-permute-start(f32[512,129]{0,1:T(8,128)S(1)} %get-tuple-element.44), channel_id=1, source_target_pairs={{0,1},{1,2},{2,3},{3,4},{4,5},{5,6},{6,7},{7,8},{8,9},{9,10},{10,1... | collective-permute-start | bytes 792584 | tf_op jit(solution)/shard_map/ppermute | solution.py:21
  177.2 7.9 %collective-permute-start.1 = (f32[512,129]{0,1:T(8,128)S(1)}, f32[512,129]{0,1:T(8,128)S(1)}, u32[]{:S(2)}, u32[]{:S(2)}) collective-permute-start(f32[512,129]{0,1:T(8,128)S(1)} %get-tuple-element.43), channel_id=1, source_target_pairs={{1,0},{2,1},{3,2},{4,3},{5,4},{6,5},{7,6},{8,7},{9,8},{10,9},{11,1... | collective-permute-start | bytes 792584 | tf_op jit(solution)/shard_map/ppermute | solution.py:23
  229.1 9.2 %copy-start = (f32[128,6912]{0,1:T(8,128)S(1)}, f32[128,6912]{0,1:T(8,128)}, u32[]{:S(2)}) copy-start(f32[128,6912]{0,1:T(8,128)} %get-tuple-element.41) | copy-start | bytes 10616836
  229.1 17.2 %copy-start.2 = (f32[512,9,512]{2,0,1:T(8,128)S(1)}, f32[512,9,512]{2,0,1:T(8,128)}, u32[]{:S(2)}) copy-start(f32[512,9,512]{2,0,1:T(8,128)} %all-gather.2.cloned.1.call-done) | copy-start | bytes 28311556
  246.2 6.5 %copy-start.1 = (f32[128,6912]{0,1:T(8,128)S(1)}, f32[128,6912]{0,1:T(8,128)}, u32[]{:S(2)}) copy-start(f32[128,6912]{0,1:T(8,128)} %get-tuple-element.39) | copy-start | bytes 10616836
  246.3 6.5 %copy-start.5 = (f32[512]{0:T(512)S(1)}, f32[512]{0:T(512)}, u32[]{:S(2)}) copy-start(f32[512]{0:T(512)} %param.11) | copy-start | bytes 6148
  343.6 74.3 %copy-start.9 = (f32[512]{0:T(512)S(1)}, f32[512]{0:T(512)}, u32[]{:S(2)}) copy-start(f32[512]{0:T(512)} %param.15) | copy-start | bytes 6148
  343.6 74.3 %copy-start.10 = (f32[512]{0:T(512)S(1)}, f32[512]{0:T(512)}, u32[]{:S(2)}) copy-start(f32[512]{0:T(512)} %param.14) | copy-start | bytes 6148
Sparse Core Ops, SparseCore 0:
  9.9 107.2 all-gather.1
where the time goes:
time: 433 us; the launch traced here: 427 us
  blocking collectives  312 us (72%)
  matrix products  42.7 us (10%)
  local copies, waits for them, and re-layouts  35.8 us (8%)
  between operations  14 us (3%)
  other arithmetic  13.9 us (3%)
  starting transfers between devices  5.59 us (1%)
    psum x2, blocking collectives, normalize(): group_total = lax.psum(group_table(firsts), ('tiles', 'sub'))  166 us
    psum x2, blocking collectives, normalize(): spread = lax.psum(group_table(seconds), ('tiles', 'sub')) / entries  146 us
    dot_general x4, matrix products, shards(): jnp.einsum('ktp,kto->po', taps_block, weight_block, precision=highest, pr...  30 us
    gather x1, local copies, waits for them, and re-layouts, shards(): tapped = jnp.take(padded, all_sources, axis=1) * all_masks[None, :]  18.6 us
    mul x1, other arithmetic, shards(): tapped = jnp.take(padded, all_sources, axis=1) * all_masks[None, :]  11.6 us
    dynamic_slice x1, local copies, waits for them, and re-layouts, shards(): taps_block = lax.dynamic_slice_in_dim(tapped, block_start, block_rows, 0)  9.35 us
  transfers between devices with their start and end apart: 3, of which 1 were waited for; matrix products, arithmetic and copies ran while one was open for 13% of the time, Pallas kernels for 0%

commit v1 on v0

--- a/solution.py
+++ b/solution.py
@@ -79,7 +79,7 @@
     seconds = jnp.dot(
         onehot, centred * centred, precision=highest, preferred_element_type=jnp.float32
     )
-    spread = lax.psum(group_table(seconds), ("tiles", "sub")) / entries
+    spread = lax.psum(lax.psum(group_table(seconds), "sub"), "tiles") / entries
     inverse = spread_rows(onehot, jnp.repeat(lax.rsqrt(spread + epsilon), group_size, axis=1))
     return jax.nn.silu(centred * inverse * norm_gain + norm_shift)
 

time: 433 us -> 615 us (1.42)
  the two profiles are of different devices: /device:TPU:1 before, /device:TPU:0 now
where the time goes in v1:
time: 615 us; the launch traced here: 606 us
  blocking collectives  496 us (81%)
  matrix products  42.7 us (7%)
  local copies, waits for them, and re-layouts  35.8 us (6%)
  other arithmetic  14.3 us (2%)
  between operations  14.1 us (2%)
    psum x4, blocking collectives, normalize(): spread = lax.psum(lax.psum(group_table(seconds), 'sub'), 'tiles') / entries  326 us
    psum x2, blocking collectives, normalize(): group_total = lax.psum(group_table(firsts), ('tiles', 'sub'))  170 us
    dot_general x4, matrix products, shards(): jnp.einsum('ktp,kto->po', taps_block, weight_block, precision=highest, pr...  30 us
    gather x1, local copies, waits for them, and re-layouts, shards(): tapped = jnp.take(padded, all_sources, axis=1) * all_masks[None, :]  18.6 us
  transfers between devices with their start and end apart: 3, of which 0 were waited for; matrix products, arithmetic and copies ran while one was open for 9% of the time, Pallas kernels for 0%

profile of v1, /device:TPU:0, one launch (start us, length us, event | category | flops | bytes accessed | tf_op | source)
XLA Modules:
  0.0 605.9 jit_solution(7930972642001056819)
XLA Ops:
  6.5 0.7 all-gather.2.cloned.1.call-update
  7.3 0.7 broadcast_multiply_fusion
  8.2 0.7 fusion.25
  8.9 2.9 bitcast_reduce_fusion.3
  11.7 81.9 %psum.42 = f32[36,32]{0,1:T(8,128)S(1)} all-reduce(f32[36,32]{0,1:T(8,128)S(1)} %bitcast_reduce_fusion.3), channel_id=1, replica_groups=mesh['tiles'=32,'sub'=8] {'tiles','sub'}, use_global_device_ids=true, to_apply=%region_5.6 | all-reduce | flops 1152 | bytes 9216 | tf_op jit(solution)/shard_map/psum | solution.py:76
  93.7 0.9 convolution_subtract_fusion.1
  94.6 1.4 bitcast_reduce_fusion.2
  96.1 24.8 %psum.43 = f32[36,32]{0,1:T(8,128)S(1)} all-reduce(f32[36,32]{0,1:T(8,128)S(1)} %bitcast_reduce_fusion.2), channel_id=1, replica_groups=mesh['tiles'=32,'sub'=8] {'sub'}, use_global_device_ids=true, to_apply=%region_7.8 | all-reduce | flops 1152 | bytes 9216 | tf_op jit(solution)/shard_map/psum | solution.py:82
  120.8 138.8 %psum.44 = f32[36,32]{0,1:T(8,128)S(1)} all-reduce(f32[36,32]{0,1:T(8,128)S(1)} %psum.43), channel_id=1, replica_groups=mesh['tiles'=32,'sub'=8] {'tiles'}, use_global_device_ids=true, to_apply=%region_8.9 | all-reduce | flops 1152 | bytes 9216 | tf_op jit(solution)/shard_map/psum | solution.py:82
  259.7 1.3 multiply_bitcast_fusion.1
  261.0 1.1 copy-done.4
  262.2 1.3 collective-permute-start
  263.5 1.3 collective-permute-start.1
  265.1 0.2 dynamic-update-slice
  265.4 0.2 dynamic-update-slice.1
  266.0 0.2 dynamic-update-slice.3
  266.9 0.2 dynamic-update-slice.6
  267.7 4.5 concatenate.54
  272.2 18.6 %gather_fusion = f32[6912,512]{1,0:T(8,128)} fusion(f32[512,1026]{0,1:T(8,128)S(1)} %concatenate.54, s32[7168]{0:T(1024)S(1)} %pad_clamp_fusion), kind=kCustom, calls=%fused_computation | custom fusion | bytes 28339200 | tf_op jit(solution)/shard_map/jit(_take)/gather | solution.py:116
  290.7 12.1 %multiply_bitcast_fusion = f32[512,6912]{0,1:T(8,128)} fusion(f32[6912,512]{1,0:T(8,128)} %gather_fusion, f32[6912]{0:T(1024)S(1)} %concatenate.66, pred[6912]{0:T(1024)(128)(4,1)S(1)} %compare_and_fusion.1), kind=kLoop, calls=%fused_computation.1 | loop fusion | flops 7077888 | bytes 28346112 | tf_op jit(solution)/shard_map/mul | solution.py:116
  302.8 9.4 %fusion.35 = (f32[128,6912]{0,1:T(8,128)}, f32[128,6912]{0,1:T(8,128)}, f32[128,6912]{0,1:T(8,128)}, f32[128,6912]{0,1:T(8,128)S(1)}) fusion(f32[512,6912]{0,1:T(8,128)} %multiply_bitcast_fusion), kind=kLoop, calls=%fused_computation.106 | loop fusion | bytes 28311552 | tf_op jit(solution)/shard_map/dynamic_slice | solution.py:124
  312.2 9.2 %fusion = f32[768,512,1]{1,0,2:T(8,128)S(1)} fusion(f32[128,9,768]{0,2,1:T(8,128)} %bitcast.48, f32[512,9,512]{2,0,1:T(8,128)} %all-gather.2.cloned.1.call-done), kind=kOutput, calls=%fused_computation.2 | convolution fusion | flops 5435817984 | bytes 7471104 | tf_op jit(solution)/shard_map/ktp,kto->po/dot_general | solution.py:127
  321.4 8.0 %fusion.2 = f32[768,512,1]{1,0,2:T(8,128)S(1)} fusion(f32[128,9,768]{0,2,1:T(8,128)S(1)} %bitcast.47, f32[512,9,512]{2,0,1:T(8,128)} %all-gather.2.cloned.1.call-done), kind=kOutput, calls=%fused_computation.4 | convolution fusion | flops 5435817984 | bytes 7471104 | tf_op jit(solution)/shard_map/ktp,kto->po/dot_general | solution.py:127
  329.4 6.5 %fusion.4 = f32[768,512,1]{1,0,2:T(8,128)S(1)} fusion(f32[128,9,768]{0,2,1:T(8,128)S(1)} %bitcast.46, f32[512,9,512]{2,0,1:T(8,128)S(1)} %copy-done.2), kind=kOutput, calls=%fused_computation.6 | convolution fusion | flops 5435817984 | bytes 7471104 | tf_op jit(solution)/shard_map/ktp,kto->po/dot_general | solution.py:127
  335.9 6.4 %fusion.8 = f32[768,512]{1,0:T(8,128)S(1)} fusion(f32[768,512,1]{1,0,2:T(8,128)S(1)} %fusion, f32[768,512,1]{1,0,2:T(8,128)S(1)} %fusion.2, f32[768,512,1]{1,0,2:T(8,128)S(1)} %fusion.4, f32[128,9,768]{0,2,1:T(8,128)S(1)} %bitcast.49, f32[512,9,512]{2,0,1:T(8,128)S(1)} %copy-done.2, f32[512]{0:T(512)S(1)} %copy-done.5), kind=kOutput, calls=%fused_computation.11 | convolution fusion | flops 5437390848 | bytes 12191744 | tf_op jit(solution)/shard_map/ktp,kto->po/dot_general | solution.py:127
  342.3 1.4 bitcast_reduce_fusion.1
  343.7 88.0 %psum.45 = f32[36,32]{0,1:T(8,128)S(1)} all-reduce(f32[36,32]{0,1:T(8,128)S(1)} %bitcast_reduce_fusion.1), channel_id=1, replica_groups=mesh['tiles'=32,'sub'=8] {'tiles','sub'}, use_global_device_ids=true, to_apply=%region_10.11 | all-reduce | flops 1152 | bytes 9216 | tf_op jit(solution)/shard_map/psum | solution.py:76
  431.8 0.9 convolution_subtract_fusion
  432.7 1.4 bitcast_reduce_fusion
  434.2 23.6 %psum.46 = f32[36,32]{0,1:T(8,128)S(1)} all-reduce(f32[36,32]{0,1:T(8,128)S(1)} %bitcast_reduce_fusion), channel_id=1, replica_groups=mesh['tiles'=32,'sub'=8] {'sub'}, use_global_device_ids=true, to_apply=%region_12.13 | all-reduce | flops 1152 | bytes 9216 | tf_op jit(solution)/shard_map/psum | solution.py:82
  457.7 138.6 %psum.47 = f32[36,32]{0,1:T(8,128)S(1)} all-reduce(f32[36,32]{0,1:T(8,128)S(1)} %psum.46), channel_id=1, replica_groups=mesh['tiles'=32,'sub'=8] {'tiles'}, use_global_device_ids=true, to_apply=%region_13.14 | all-reduce | flops 1152 | bytes 9216 | tf_op jit(solution)/shard_map/psum | solution.py:82
  596.4 2.4 divide_multiply_fusion
  (71 shorter events, 2.3 us)
Async XLA Ops:
  6.5 87.1 %copy-start.3 = (f32[768,512]{1,0:T(8,128)S(1)}, f32[768,512]{1,0:T(8,128)}, u32[]{:S(2)}) copy-start(f32[768,512]{1,0:T(8,128)} %param.9) | copy-start | bytes 4718596
  6.5 305.6 %all-gather.2.cloned.1.call-start = ((), (), s32[]{:S(2)}) async-start(), calls=%async_computation | async-start | bytes 9732096 | tf_op jit(solution)/shard_map/all_gather | solution.py:119
  94.6 165.1 %copy-start.7 = (f32[512]{0:T(512)S(1)}, f32[512]{0:T(512)}, u32[]{:S(2)}) copy-start(f32[512]{0:T(512)} %param.13) | copy-start | bytes 6148
  94.6 165.1 %copy-start.8 = (f32[512]{0:T(512)S(1)}, f32[512]{0:T(512)}, u32[]{:S(2)}) copy-start(f32[512]{0:T(512)} %param.12) | copy-start | bytes 6148
  259.7 5.1 copy-start.6
  261.0 1.1 copy-start.4
  262.2 5.5 collective-permute-start
  263.5 4.2 collective-permute-start.1
  312.2 9.2 %copy-start = (f32[128,6912]{0,1:T(8,128)S(1)}, f32[128,6912]{0,1:T(8,128)}, u32[]{:S(2)}) copy-start(f32[128,6912]{0,1:T(8,128)} %get-tuple-element.41) | copy-start | bytes 10616836
  312.2 17.2 %copy-start.2 = (f32[512,9,512]{2,0,1:T(8,128)S(1)}, f32[512,9,512]{2,0,1:T(8,128)}, u32[]{:S(2)}) copy-start(f32[512,9,512]{2,0,1:T(8,128)} %all-gather.2.cloned.1.call-done) | copy-start | bytes 28311556
  329.4 6.5 %copy-start.1 = (f32[128,6912]{0,1:T(8,128)S(1)}, f32[128,6912]{0,1:T(8,128)}, u32[]{:S(2)}) copy-start(f32[128,6912]{0,1:T(8,128)} %get-tuple-element.39) | copy-start | bytes 10616836
  329.4 6.5 %copy-start.5 = (f32[512]{0:T(512)S(1)}, f32[512]{0:T(512)}, u32[]{:S(2)}) copy-start(f32[512]{0:T(512)} %param.11) | copy-start | bytes 6148
  432.7 163.7 %copy-start.9 = (f32[512]{0:T(512)S(1)}, f32[512]{0:T(512)}, u32[]{:S(2)}) copy-start(f32[512]{0:T(512)} %param.15) | copy-start | bytes 6148
  432.7 163.7 %copy-start.10 = (f32[512]{0:T(512)S(1)}, f32[512]{0:T(512)}, u32[]{:S(2)}) copy-start(f32[512]{0:T(512)} %param.14) | copy-start | bytes 6148
Sparse Core Ops, SparseCore 0:
  9.9 105.2 all-gather.1
